TPU v7x, 32 devices: a whole 2x2x4 slice. The times are simulated.
32 devices in a mesh: grp: 2 (over y), row: 4 (over z), col: 2 (over x), sub: 2 (over core).
Axes of the slice: x: 2, y: 2, z: 4, core: 2. Of those that a mesh axis runs over, the one named last changes fastest.
Arguments:
- pair: bfloat16 [96, 48, 128], P(('grp', 'row'), 'col'), parts along dimension 0, may hold values from -6 to 6
- length: int32 [2], P('grp'), parts along dimension 0, may hold values from 24 to 48
- chain: int32 [96], P('grp'), parts along dimension 0, may hold values from 0 to 3, never falling along the last dimension, each value on 1 to 24 neighbouring positions
- att_proj: bfloat16 [128, 4, 128], P(None, None, 'sub'), may hold values from -0.5 to 0.5
- att_bias: bfloat16 [128, 4], P(None, 'sub')
- chain_bias: float32 [4], P('sub'), may hold values from -2 to 2
- att_out: bfloat16 [128, 128], P('sub'), may hold values from -0.5 to 0.5
- mult_in: bfloat16 [128, 512], replicated, may hold values from -0.5 to 0.5
- mult_gate: bfloat16 [128, 128], replicated, may hold values from -0.5 to 0.5
- mult_out: bfloat16 [128, 128], replicated, may hold values from -0.5 to 0.5
- trans_up: bfloat16 [128, 512], replicated, may hold values from -0.5 to 0.5
- trans_down: bfloat16 [512, 128], replicated, may hold values from -0.25 to 0.25
Outputs:
- pair_out: bfloat16 [96, 48, 128], P(('grp', 'row'), ('col', 'sub')), parts along dimension 0
There are 2 independent parts, one for each index of `grp`. A program takes and returns all parts, laid end to end along the dimension named above; an argument that names none is the same for every part. Nothing has to cross between parts.
Inputs may be any that keep to these rules, and one draw needn't show every extreme that they name: chain numbers never fall along the residues; each chain has 1 to 24 residues.
All inputs are finite; a program needn't handle non-finite values.
Results may differ from a plain program's by a relative error of at most 0.012.
The roundings to bfloat16 on the way count: a program that leaves them out, or rounds other values in their place, can miss the bound.
Values may be sent and summed in bfloat16 or wider, within the bound.
No kernel may reach another device: no remote copies, remote signals or barrier semaphores. Data moves between devices by JAX's collectives and lax.ppermute only.
A program may use at most 64 MiB of HBM per device.

v0:
```python
import jax
import jax.numpy as jnp
from jax import lax
from jax.sharding import PartitionSpec as P


def norm(value):
    mean = jnp.mean(value, axis=-1, keepdims=True)
    centred = value - mean
    variance = jnp.mean(centred * centred, axis=-1, keepdims=True)
    return centred * lax.rsqrt(variance + 1e-05)


def local(
    pair,
    length,
    chain,
    att_proj,
    att_bias,
    chain_bias,
    att_out,
    mult_in,
    mult_gate,
    mult_out,
    trans_up,
    trans_down,
):
    rows, cols, width = pair.shape
    row_count = lax.axis_size("row")
    sub_count = lax.axis_size("sub")
    row_index = lax.axis_index("row")
    col_index = lax.axis_index("col")
    sub_index = lax.axis_index("sub")
    total = rows * row_count
    half = cols // sub_count
    heads_here = att_bias.shape[1]
    spread = att_out.shape[0]
    head_dim = spread // heads_here
    mult_width = mult_out.shape[0]
    valid = (jnp.arange(total) < length[0]).astype(jnp.float32)
    normed = norm(pair.astype(jnp.float32)).astype(jnp.bfloat16)
    flat = normed.reshape(rows * cols, width)
    projected = jnp.dot(
        flat, att_proj.reshape(width, 4 * spread), preferred_element_type=jnp.float32
    ).reshape(rows, cols, 4, spread)
    query = (projected[:, :, 0] * head_dim ** (-0.5)).astype(jnp.bfloat16)
    keys = projected[:, :, 1].astype(jnp.bfloat16)
    values = projected[:, :, 2].astype(jnp.bfloat16)
    gating = jax.nn.sigmoid(projected[:, :, 3])
    bias_local = (
        jnp.dot(flat, att_bias, preferred_element_type=jnp.float32)
        .reshape(rows, cols, heads_here)
        .transpose(2, 0, 1)
    )
    keys_all, values_all = (
        lax.all_gather(keys, "col", axis=1, tiled=True),
        lax.all_gather(values, "col", axis=1, tiled=True),
    )
    column_bias = lax.all_gather(bias_local, "row", axis=1, tiled=True)
    bias_here = lax.all_to_all(column_bias, "col", split_axis=1, concat_axis=2, tiled=True)
    chain_here = lax.dynamic_slice_in_dim(chain, col_index * cols, cols, 0)
    same = (chain_here[:, None] == chain[None, :]).astype(jnp.float32)
    bias_here = (
        bias_here
        + chain_bias[:, None, None] * same[None]
        + (valid[None, None, :] - 1.0) * 1000000000.0
    )

    def attend(block):
        block_query, block_keys, block_values = block
        scores = (
            jnp.einsum(
                "ajhd,akhd->ahjk", block_query, block_keys, preferred_element_type=jnp.float32
            )
            + bias_here[None]
        )
        weights = jax.nn.softmax(scores, axis=-1).astype(jnp.bfloat16)
        return jnp.einsum(
            "ahjk,akhd->ajhd", weights, block_values, preferred_element_type=jnp.float32
        )

    attended = lax.map(
        attend,
        (
            query.reshape(rows // 2, 2, cols, heads_here, head_dim),
            keys_all.reshape(rows // 2, 2, total, heads_here, head_dim),
            values_all.reshape(rows // 2, 2, total, heads_here, head_dim),
        ),
    )
    attended = (attended.reshape(rows, cols, spread) * gating).astype(jnp.bfloat16)
    update = jnp.dot(
        attended.reshape(rows * cols, spread), att_out, preferred_element_type=jnp.float32
    ).reshape(rows, cols, width)
    update_half = lax.psum_scatter(
        update.astype(jnp.bfloat16), "sub", scatter_dimension=1, tiled=True
    ).astype(jnp.float32)
    pair_half = lax.dynamic_slice_in_dim(pair, sub_index * half, half, 1).astype(jnp.float32)
    first = pair_half + update_half
    mixed = norm(first).astype(jnp.bfloat16)
    mixed_flat = mixed.reshape(rows * half, width)
    quad = jnp.dot(mixed_flat, mult_in, preferred_element_type=jnp.float32).reshape(
        rows, half, 4, mult_width
    )
    row_valid = lax.dynamic_slice_in_dim(valid, row_index * rows, rows, 0)
    col_valid = lax.dynamic_slice_in_dim(valid, col_index * cols + sub_index * half, half, 0)
    outer = row_valid[:, None, None] * col_valid[None, :, None]
    left = (outer * jax.nn.sigmoid(quad[:, :, 1]) * quad[:, :, 0]).astype(jnp.bfloat16)
    right = (outer * jax.nn.sigmoid(quad[:, :, 3]) * quad[:, :, 2]).astype(jnp.bfloat16)
    gate_out = jax.nn.sigmoid(jnp.dot(mixed_flat, mult_gate, preferred_element_type=jnp.float32))
    partial_value = jnp.einsum(
        "ikc,jkc->ijc",
        left,
        lax.all_gather(right, "row", axis=0, tiled=True),
        preferred_element_type=jnp.float32,
    )
    tri = lax.psum_scatter(
        partial_value.astype(jnp.bfloat16), ("col", "sub"), scatter_dimension=1, tiled=True
    ).astype(jnp.float32)
    tri_normed = norm(tri).astype(jnp.bfloat16).reshape(rows * half, mult_width)
    second = first + (
        gate_out * jnp.dot(tri_normed, mult_out, preferred_element_type=jnp.float32)
    ).reshape(rows, half, width)
    last_normed = norm(second).astype(jnp.bfloat16).reshape(rows * half, width)
    hidden = jax.nn.relu(jnp.dot(last_normed, trans_up, preferred_element_type=jnp.float32)).astype(
        jnp.bfloat16
    )
    result = second + jnp.dot(hidden, trans_down, preferred_element_type=jnp.float32).reshape(
        rows, half, width
    )
    return result.astype(jnp.bfloat16)


def solution(mesh):
    placed = (
        P(("grp", "row"), "col", None),
        P("grp"),
        P("grp"),
        P(None, None, "sub"),
        P(None, "sub"),
        P("sub"),
        P("sub", None),
        P(),
        P(),
        P(),
        P(),
        P(),
    )
    return jax.shard_map(
        local,
        mesh=mesh,
        in_specs=placed,
        out_specs=P(("grp", "row"), ("col", "sub"), None),
        check_vma=False,
    )
```

profile of v0, /device:TPU:0, one launch (start us, length us, event | category | flops | bytes accessed | tf_op | source)
XLA Modules:
  0.0 124.0 jit_solution(8940343694213639194)
XLA Ops:
  6.5 1.0 convert_reduce_fusion
  7.6 1.1 fusion.21
  8.7 1.2 convolution_bitcast_fusion.1
  9.9 14.8 %all_gather.14 = f32[2,48,24]{2,0,1:T(2,128)S(1)} all-gather(f32[2,12,24]{2,0,1:T(2,128)S(1)} %convolution_bitcast_fusion.1), channel_id=1, replica_groups=mesh['grp'=2,'row'=4,'col'=2,'sub'=2] {'row'}, dimensions={1}, use_global_device_ids=true | all-gather | bytes 11520 | tf_op jit(solution)/shard_map/all_gather | solution.py:59
  24.6 0.7 reshape.214
  25.4 3.2 %all-to-all-start = ((f32[2,1,1152]{2,1,0:T(1,128)}), f32[2,1,1152]{2,1,0:T(1,128)S(1)}, u32[]{:S(2)}, u32[]{:S(2)}) async-start(f32[2,1,1152]{2,1,0:T(1,128)} %reshape.214), calls=%async_computation | async-start | bytes 18432 | tf_op jit(solution)/shard_map/all_to_all | solution.py:60
  28.7 0.7 dynamic_slice.24
  29.4 0.7 compare_convert_fusion
  30.8 1.2 fusion.72
  32.0 5.4 %all-gather = bf16[12,48,1,64]{3,1,2,0:T(8,128)(2,1)S(1)} all-gather(bf16[12,24,1,64]{3,1,2,0:T(8,128)(2,1)S(1)} %get-tuple-element.85), channel_id=2, replica_groups=mesh['grp'=2,'row'=4,'col'=2,'sub'=2] {'col'}, dimensions={1}, use_global_device_ids=true | all-gather | bytes 110592 | tf_op jit(solution)/shard_map/all_gather | solution.py:57
  37.6 5.2 %all-gather.1 = bf16[12,48,1,64]{3,1,2,0:T(8,128)(2,1)S(1)} all-gather(bf16[12,24,1,64]{3,1,2,0:T(8,128)(2,1)S(1)} %get-tuple-element.84), channel_id=3, replica_groups=mesh['grp'=2,'row'=4,'col'=2,'sub'=2] {'col'}, dimensions={1}, use_global_device_ids=true | all-gather | bytes 110592 | tf_op jit(solution)/shard_map/all_gather | solution.py:56
  43.2 0.5 broadcast.191
  43.7 0.7 reduce
  44.8 4.9 %while.10 = (s32[]{:T(128)}, f32[6,2,24,2,32]{4,3,2,1,0:T(2,128)S(1)}, bf16[6,2,48,2,32]{2,4,3,1,0:T(8,128)(2,1)S(1)}, bf16[6,2,24,2,32]{4,3,2,1,0:T(2,128)(2,1)...) while((s32[]{:T(128)}, f32[6,2,24,2,32]{4,3,2,1,0:T(2,128)S(1)}, ...), condition=%wide.region_5.6_spmd, body=%wide.region_2.5_spmd.sunk | while | flops 917184 | bytes 438753 | solution.py:82
  47.4 0.3 fusion.93
  48.2 0.3 fusion.93
  49.9 0.8 convolution_convert_fusion.1
  51.0 0.6 dynamic-slice
  52.2 17.7 %all-reduce.3.cloned.1.call-done = bf16[12,24,128]{2,1,0:T(8,128)(2,1)} async-done(((bf16[12,24,128]{2,1,0:T(8,128)(2,1)}), bf16[12,24,128]{2,1,0:T(8,128)(2,1)}) %all-reduce.3.cloned.1.call-update) | async-done | bytes 73744
  69.9 1.0 fusion.52
  71.0 1.1 multiply_reduce_fusion.1
  72.1 1.0 multiply_convert_fusion.1
  73.4 14.1 %all_gather.15 = bf16[48,12,128]{2,1,0:T(8,128)(2,1)S(1)} all-gather(bf16[12,12,128]{2,1,0:T(8,128)(2,1)S(1)} %get-tuple-element.83), channel_id=1, replica_groups=mesh['grp'=2,'row'=4,'col'=2,'sub'=2] {'row'}, dimensions={0}, use_global_device_ids=true | all-gather | bytes 184320 | tf_op jit(solution)/shard_map/all_gather | solution.py:113
  87.5 1.0 copy.77
  88.5 0.5 copy.78
  89.0 0.9 fusion.13
  89.9 1.2 copy.79
  91.4 20.9 %reduce-scatter.3.cloned.1.call-done = bf16[12,12,128]{2,0,1:T(8,128)(2,1)} async-done(((bf16[12,48,128]{2,0,1:T(8,128)(2,1)}), bf16[12,12,128]{2,0,1:T(8,128)(2,1)}) %reduce-scatter.3.cloned.1.call-update) | async-done | bytes 36880 | tf_op jit(solution)/shard_map/reduce_scatter | solution.py:116
  112.3 0.9 convert_reduce_fusion.1
  113.4 1.0 fusion.33
  114.6 0.9 fusion.34
  116.6 0.6 add_convert_fusion
  (95 shorter events, 7.4 us)
Async XLA Ops:
  6.5 109.7 %copy-start = (bf16[512,128]{1,0:T(8,128)(2,1)S(1)}, bf16[512,128]{1,0:T(8,128)(2,1)}, u32[]{:S(2)}) copy-start(bf16[512,128]{1,0:T(8,128)(2,1)} %param.25) | copy-start | bytes 393220
  25.4 17.8 %all-to-all-start = ((f32[2,1,1152]{2,1,0:T(1,128)}), f32[2,1,1152]{2,1,0:T(1,128)S(1)}, u32[]{:S(2)}, u32[]{:S(2)}) async-start(f32[2,1,1152]{2,1,0:T(1,128)} %reshape.214), calls=%async_computation | async-start | bytes 18432 | tf_op jit(solution)/shard_map/all_to_all | solution.py:60
  28.6 41.3 %all-reduce.3.cloned.1.call-start = ((), (), s32[]{:S(2)}) async-start(), calls=%async_computation.3 | async-start | bytes 147456
  30.8 13.9 %copy-start.6 = (f32[2]{0:T(128)S(1)}, f32[2]{0:T(128)}, u32[]{:S(2)}) copy-start(f32[2]{0:T(128)} %param.19) | copy-start | bytes 28
  44.8 5.1 %copy-start.8 = (bf16[64,128]{1,0:T(8,128)(2,1)S(1)}, bf16[64,128]{1,0:T(8,128)(2,1)}, u32[]{:S(2)}) copy-start(bf16[64,128]{1,0:T(8,128)(2,1)} %param.20) | copy-start | bytes 49156
  44.8 6.1 %copy-start.4 = (bf16[128,512]{1,0:T(8,128)(2,1)S(1)}, bf16[128,512]{1,0:T(8,128)(2,1)}, u32[]{:S(2)}) copy-start(bf16[128,512]{1,0:T(8,128)(2,1)} %param.21) | copy-start | bytes 393220
  44.8 6.2 %copy-start.9 = (u32[32]{0:T(128)S(1)}, u32[32]{0:T(128)}, u32[]{:S(2)}) copy-start(u32[32]{0:T(128)} %constant.70) | copy-start | bytes 388
  49.7 20.3 %copy-start.1 = (bf16[12,24,128]{2,1,0:T(8,128)(2,1)S(1)}, bf16[12,24,128]{2,1,0:T(8,128)(2,1)}, u32[]{:S(2)}) copy-start(bf16[12,24,128]{2,1,0:T(8,128)(2,1)} %param.14) | copy-start | bytes 221188
  50.7 61.6 %reduce-scatter.3.cloned.1.call-start = ((), (), s32[]{:S(2)}) async-start(), calls=%async_computation.2 | async-start | bytes 245760 | tf_op jit(solution)/shard_map/reduce_scatter | solution.py:116
  89.0 2.2 %copy-start.7 = (bf16[128,128]{1,0:T(8,128)(2,1)S(1)}, bf16[128,128]{1,0:T(8,128)(2,1)}, u32[]{:S(2)}) copy-start(bf16[128,128]{1,0:T(8,128)(2,1)} %param.22) | copy-start | bytes 98308
  89.9 25.7 %copy-start.5 = (bf16[128,128]{1,0:T(8,128)(2,1)S(1)}, bf16[128,128]{1,0:T(8,128)(2,1)}, u32[]{:S(2)}) copy-start(bf16[128,128]{1,0:T(8,128)(2,1)} %param.23) | copy-start | bytes 98308
  89.9 25.8 %copy-start.2 = (bf16[12,24,128]{2,1,0:T(8,128)(2,1)S(1)}, bf16[12,24,128]{2,1,0:T(8,128)(2,1)}, u32[]{:S(2)}) copy-start(bf16[12,24,128]{2,1,0:T(8,128)(2,1)} %all-reduce.3.cloned.1.call-done) | copy-start | bytes 221188
  89.9 26.3 %copy-start.3 = (bf16[128,512]{1,0:T(8,128)(2,1)S(1)}, bf16[128,512]{1,0:T(8,128)(2,1)}, u32[]{:S(2)}) copy-start(bf16[128,512]{1,0:T(8,128)(2,1)} %param.24) | copy-start | bytes 393220
Sparse Core Ops, SparseCore 0:
  50.8 19.0 all-reduce.2
  91.3 20.9 reduce-scatter.2
where the time goes:
time: 125 us; the launch traced here: 124 us
  blocking collectives  39.5 us (32%)
  waiting for transfers between devices  38.7 us (31%)
  between operations  15.2 us (12%)
  other arithmetic  10.7 us (9%)
  matrix products  9.25 us (7%)
  local copies, waits for them, and re-layouts  7.19 us (6%)
  starting transfers between devices  3.31 us (3%)
    reduce_scatter x1, waiting for transfers between devices, local(): lax.psum_scatter(partial_value.astype(jnp.bfloat16), ('col', 'sub'), scat...  20.9 us
    unnamed x3, waiting for transfers between devices  17.8 us
    all_gather x1, blocking collectives, local(): column_bias = lax.all_gather(bias_local, 'row', axis=1, tiled=True)  14.8 us
    all_gather x1, blocking collectives, local(): lax.all_gather(right, 'row', axis=0, tiled=True)  14.1 us
    all_gather x1, blocking collectives, local(): lax.all_gather(values, 'col', axis=1, tiled=True)  5.44 us
    all_gather x1, blocking collectives, local(): lax.all_gather(keys, 'col', axis=1, tiled=True)  5.2 us
    reduce_sum x4, other arithmetic, norm(): variance = jnp.mean(centred * centred, axis=-1, keepdims=True)  3.31 us
    all_to_all x1, starting transfers between devices, local(): lax.all_to_all(column_bias, 'col', split_axis=1, concat_axis=2, tiled=True)  3.23 us
  transfers between devices with their start and end apart: 3, of which 2 were waited for; matrix products, arithmetic and copies ran while one was open for 3% of the time, Pallas kernels for 0%

commit v1 on v0

--- a/solution.py
+++ b/solution.py
@@ -56,7 +56,12 @@
         lax.all_gather(keys, "col", axis=1, tiled=True),
         lax.all_gather(values, "col", axis=1, tiled=True),
     )
-    column_bias = lax.all_gather(bias_local, "row", axis=1, tiled=True)
+    ring = [bias_local]
+    for hop in range(3):
+        ring.append(lax.ppermute(ring[-1], "row", [(dev, (dev + 1) % 4) for dev in range(4)]))
+    column_bias = jnp.roll(
+        jnp.concatenate(ring[::-1], axis=1), (lax.axis_index("row") + 1) * ring[0].shape[1], axis=1
+    )
     bias_here = lax.all_to_all(column_bias, "col", split_axis=1, concat_axis=2, tiled=True)
     chain_here = lax.dynamic_slice_in_dim(chain, col_index * cols, cols, 0)
     same = (chain_here[:, None] == chain[None, :]).astype(jnp.float32)

time: 125 us -> 119 us (0.952)
  blocking collectives: 39.5 us -> 24.1 us
  waiting for transfers between devices: 38.7 us -> 43.9 us
  starting transfers between devices: 3.31 us -> 7.72 us
    all_gather x1 -> x0, blocking collectives: 14.8 us -> none  [local(): column_bias = lax.all_gather(bias_local, 'row', axis=1, tiled=True)]
    ppermute x0 -> x3, waiting for transfers between devices: none -> 4.87 us  [local(): lax.ppermute(ring[-1], 'row', [(dev, (dev + 1) % 4) for dev in range(4)])]
    ppermute x0 -> x3, starting transfers between devices: none -> 4.41 us  [local(): lax.ppermute(ring[-1], 'row', [(dev, (dev + 1) % 4) for dev in range(4)])]
  transfers between devices with their start and end apart: 3 -> 6, of which waited for: 2 -> 5; matrix products, arithmetic and copies ran while one was open for 3% -> 3% of each run, Pallas kernels for 0% -> 0%
where the time goes in v1:
time: 119 us; the launch traced here: 118 us
  waiting for transfers between devices  43.9 us (37%)
  blocking collectives  24.1 us (20%)
  between operations  15.2 us (13%)
  other arithmetic  10.7 us (9%)
  matrix products  9.26 us (8%)
  starting transfers between devices  7.72 us (6%)
  local copies, waits for them, and re-layouts  7.26 us (6%)
    reduce_scatter x1, waiting for transfers between devices, local(): lax.psum_scatter(partial_value.astype(jnp.bfloat16), ('col', 'sub'), scat...  21 us
    unnamed x3, waiting for transfers between devices  18.1 us
    all_gather x1, blocking collectives, local(): lax.all_gather(right, 'row', axis=0, tiled=True)  14.1 us
    all_gather x1, blocking collectives, local(): lax.all_gather(keys, 'col', axis=1, tiled=True)  5.02 us
    all_gather x1, blocking collectives, local(): lax.all_gather(values, 'col', axis=1, tiled=True)  5.01 us
    ppermute x3, waiting for transfers between devices, local(): lax.ppermute(ring[-1], 'row', [(dev, (dev + 1) % 4) for dev in range(4)])  4.87 us
    ppermute x3, starting transfers between devices, local(): lax.ppermute(ring[-1], 'row', [(dev, (dev + 1) % 4) for dev in range(4)])  4.41 us
    reduce_sum x4, other arithmetic, norm(): variance = jnp.mean(centred * centred, axis=-1, keepdims=True)  3.31 us
  transfers between devices with their start and end apart: 6, of which 5 were waited for; matrix products, arithmetic and copies ran while one was open for 3% of the time, Pallas kernels for 0%

profile of v1, /device:TPU:0, one launch (start us, length us, event | category | flops | bytes accessed | tf_op | source)
XLA Modules:
  0.0 118.4 jit_solution(5342397341412451744)
XLA Ops:
  6.5 1.0 convert_reduce_fusion
  7.6 1.1 fusion.21
  8.7 1.2 %convolution_bitcast_fusion.1 = f32[2,12,24]{2,0,1:T(2,128)S(1)} fusion(bf16[12,24,128]{2,1,0:T(8,128)(2,1)} %param.14, f32[12,24]{1,0:T(8,128)S(1)} %add_rsqrt_fusion.3, f32[12,24]{1,0:T(8,128)S(1)} %broadcast_multiply_fusion.4, bf16[128,2]{0,1:T(2,128)(2,1)} %param.18), kind=kOutput, calls=%fused_computation.28 | convolution fusion | flops 294912 | bytes 78848 | tf_op jit(solution)/shard_map/dot_general | solution.py:51
  9.9 3.1 %collective-permute-start = (f32[2,12,24]{2,0,1:T(2,128)S(1)}, f32[2,12,24]{2,0,1:T(2,128)S(1)}, u32[]{:S(2)}, u32[]{:S(2)}) collective-permute-start(f32[2,12,24]{2,0,1:T(2,128)S(1)} %convolution_bitcast_fusion.1), channel_id=1, source_target_pairs={{0,4},{4,8},{8,12},{12,0},{1,5},{5,9},{9,13},{13,1},{2,6},{6,10},{... | collective-permute-start | bytes 6920 | tf_op jit(solution)/shard_map/ppermute | solution.py:61
  12.9 0.7 dynamic_slice.29
  13.7 0.7 compare_convert_fusion
  15.1 1.2 %fusion.72 = (bf16[12,24,4,64]{3,1,2,0:T(8,128)(2,1)S(1)}, f32[12,24,4,64]{3,1,2,0:T(8,128)S(1)}) fusion(bf16[128,4,64]{0,2,1:T(8,128)(2,1)} %param.17, f32[12,24]{1,0:T(8,128)S(1)} %add_rsqrt_fusion.3, f32[12,24]{1,0:T(8,128)S(1)} %broadcast_multiply_fusion.4, bf16[12,24,128]{2,1,0:T(8,128)(2,1)} %param.14), kind=kOutput, calls=%fused_computation.114 | convolution fusion | flops 19095552 | bytes 583936 | tf_op jit(solution)/shard_map/dot_general | solution.py:43
  16.6 1.3 %collective-permute-start.1 = (f32[2,12,24]{2,0,1:T(2,128)S(1)}, f32[2,12,24]{2,0,1:T(2,128)S(1)}, u32[]{:S(2)}, u32[]{:S(2)}) collective-permute-start(f32[2,12,24]{2,0,1:T(2,128)S(1)} %collective-permute-done), channel_id=1, source_target_pairs={{0,4},{4,8},{8,12},{12,0},{1,5},{5,9},{9,13},{13,1},{2,6},{6,10},{... | collective-permute-start | bytes 6920 | tf_op jit(solution)/shard_map/ppermute | solution.py:61
  18.0 4.1 %collective-permute-done.1 = f32[2,12,24]{2,0,1:T(2,128)S(1)} collective-permute-done((f32[2,12,24]{2,0,1:T(2,128)S(1)}, f32[2,12,24]{2,0,1:T(2,128)S(1)}, u32[]{:S(2)}, u32[]{:S(2)}) %collective-permute-start.1) | collective-permute-done | bytes 2336 | tf_op jit(solution)/shard_map/ppermute | solution.py:61
  22.1 5.0 %all-gather = bf16[12,48,1,64]{3,1,2,0:T(8,128)(2,1)S(1)} all-gather(bf16[12,24,1,64]{3,1,2,0:T(8,128)(2,1)S(1)} %get-tuple-element.91), channel_id=2, replica_groups=mesh['grp'=2,'row'=4,'col'=2,'sub'=2] {'col'}, dimensions={1}, use_global_device_ids=true | all-gather | bytes 110592 | tf_op jit(solution)/shard_map/all_gather | solution.py:57
  27.1 0.5 collective-permute-done.2
  27.7 0.7 reshape.214
  28.5 3.2 %all-to-all-start = ((f32[2,1,1152]{2,1,0:T(1,128)}), f32[2,1,1152]{2,1,0:T(1,128)S(1)}, u32[]{:S(2)}, u32[]{:S(2)}) async-start(f32[2,1,1152]{2,1,0:T(1,128)} %reshape.214), calls=%async_computation | async-start | bytes 18432 | tf_op jit(solution)/shard_map/all_to_all | solution.py:65
  31.7 5.0 %all-gather.1 = bf16[12,48,1,64]{3,1,2,0:T(8,128)(2,1)S(1)} all-gather(bf16[12,24,1,64]{3,1,2,0:T(8,128)(2,1)S(1)} %get-tuple-element.90), channel_id=3, replica_groups=mesh['grp'=2,'row'=4,'col'=2,'sub'=2] {'col'}, dimensions={1}, use_global_device_ids=true | all-gather | bytes 110592 | tf_op jit(solution)/shard_map/all_gather | solution.py:56
  37.2 0.5 broadcast.191
  37.7 0.7 reduce
  38.8 4.9 %while.10 = (s32[]{:T(128)}, f32[6,2,24,2,32]{4,3,2,1,0:T(2,128)S(1)}, bf16[6,2,48,2,32]{2,4,3,1,0:T(8,128)(2,1)S(1)}, bf16[6,2,24,2,32]{4,3,2,1,0:T(2,128)(2,1)...) while((s32[]{:T(128)}, f32[6,2,24,2,32]{4,3,2,1,0:T(2,128)S(1)}, ...), condition=%wide.region_5.6_spmd, body=%wide.region_2.5_spmd.sunk | while | flops 917184 | bytes 438753 | solution.py:87
  43.9 0.8 convolution_convert_fusion.1
  45.0 0.6 dynamic-slice
  46.2 18.0 %all-reduce.3.cloned.1.call-done = bf16[12,24,128]{2,1,0:T(8,128)(2,1)} async-done(((bf16[12,24,128]{2,1,0:T(8,128)(2,1)}), bf16[12,24,128]{2,1,0:T(8,128)(2,1)}) %all-reduce.3.cloned.1.call-update) | async-done | bytes 73744
  64.2 1.0 fusion.52
  65.2 1.1 multiply_reduce_fusion.1
  66.3 1.0 multiply_convert_fusion.1
  67.7 14.1 %all_gather.11 = bf16[48,12,128]{2,1,0:T(8,128)(2,1)S(1)} all-gather(bf16[12,12,128]{2,1,0:T(8,128)(2,1)S(1)} %get-tuple-element.89), channel_id=1, replica_groups=mesh['grp'=2,'row'=4,'col'=2,'sub'=2] {'row'}, dimensions={0}, use_global_device_ids=true | all-gather | bytes 184320 | tf_op jit(solution)/shard_map/all_gather | solution.py:118
  81.8 1.0 copy.120
  83.3 0.9 fusion.13
  84.2 1.2 %copy.122 = bf16[12,48,128]{2,0,1:T(8,128)(2,1)} copy(bf16[12,48,128]{1,0,2:T(8,128)(2,1)S(1)} %fusion.13) | data formatting | bytes 294912 | tf_op jit(solution)/shard_map/convert_element_type | solution.py:122
  85.6 21.0 %reduce-scatter.3.cloned.1.call-done = bf16[12,12,128]{2,0,1:T(8,128)(2,1)} async-done(((bf16[12,48,128]{2,0,1:T(8,128)(2,1)}), bf16[12,12,128]{2,0,1:T(8,128)(2,1)}) %reduce-scatter.3.cloned.1.call-update) | async-done | bytes 36880 | tf_op jit(solution)/shard_map/reduce_scatter | solution.py:121
  106.6 0.9 convert_reduce_fusion.1
  107.7 1.0 fusion.33
  108.9 0.9 fusion.34
  110.9 0.6 add_convert_fusion
  (109 shorter events, 8.7 us)
Async XLA Ops:
  6.5 104.0 %copy-start = (bf16[512,128]{1,0:T(8,128)(2,1)S(1)}, bf16[512,128]{1,0:T(8,128)(2,1)}, u32[]{:S(2)}) copy-start(bf16[512,128]{1,0:T(8,128)(2,1)} %param.25) | copy-start | bytes 393220
  9.9 6.8 %collective-permute-start = (f32[2,12,24]{2,0,1:T(2,128)S(1)}, f32[2,12,24]{2,0,1:T(2,128)S(1)}, u32[]{:S(2)}, u32[]{:S(2)}) collective-permute-start(f32[2,12,24]{2,0,1:T(2,128)S(1)} %convolution_bitcast_fusion.1), channel_id=1, source_target_pairs={{0,4},{4,8},{8,12},{12,0},{1,5},{5,9},{9,13},{13,1},{2,6},{6,10},{... | collective-permute-start | bytes 6920 | tf_op jit(solution)/shard_map/ppermute | solution.py:61
  15.0 23.6 %copy-start.6 = (f32[2]{0:T(128)S(1)}, f32[2]{0:T(128)}, u32[]{:S(2)}) copy-start(f32[2]{0:T(128)} %param.19) | copy-start | bytes 28
  16.6 5.5 %collective-permute-start.1 = (f32[2,12,24]{2,0,1:T(2,128)S(1)}, f32[2,12,24]{2,0,1:T(2,128)S(1)}, u32[]{:S(2)}, u32[]{:S(2)}) collective-permute-start(f32[2,12,24]{2,0,1:T(2,128)S(1)} %collective-permute-done), channel_id=1, source_target_pairs={{0,4},{4,8},{8,12},{12,0},{1,5},{5,9},{9,13},{13,1},{2,6},{6,10},{... | collective-permute-start | bytes 6920 | tf_op jit(solution)/shard_map/ppermute | solution.py:61
  22.1 5.5 %collective-permute-start.2 = (f32[2,12,24]{2,0,1:T(2,128)S(1)}, f32[2,12,24]{2,0,1:T(2,128)S(1)}, u32[]{:S(2)}, u32[]{:S(2)}) collective-permute-start(f32[2,12,24]{2,0,1:T(2,128)S(1)} %collective-permute-done.1), channel_id=1, source_target_pairs={{0,4},{4,8},{8,12},{12,0},{1,5},{5,9},{9,13},{13,1},{2,6},{6,10},{... | collective-permute-start | bytes 6920 | tf_op jit(solution)/shard_map/ppermute | solution.py:61
  28.5 8.7 %all-to-all-start = ((f32[2,1,1152]{2,1,0:T(1,128)}), f32[2,1,1152]{2,1,0:T(1,128)S(1)}, u32[]{:S(2)}, u32[]{:S(2)}) async-start(f32[2,1,1152]{2,1,0:T(1,128)} %reshape.214), calls=%async_computation | async-start | bytes 18432 | tf_op jit(solution)/shard_map/all_to_all | solution.py:65
  31.7 32.5 %all-reduce.3.cloned.1.call-start = ((), (), s32[]{:S(2)}) async-start(), calls=%async_computation.3 | async-start | bytes 147456
  38.7 5.1 %copy-start.8 = (bf16[64,128]{1,0:T(8,128)(2,1)S(1)}, bf16[64,128]{1,0:T(8,128)(2,1)}, u32[]{:S(2)}) copy-start(bf16[64,128]{1,0:T(8,128)(2,1)} %param.20) | copy-start | bytes 49156
  38.8 6.1 %copy-start.4 = (bf16[128,512]{1,0:T(8,128)(2,1)S(1)}, bf16[128,512]{1,0:T(8,128)(2,1)}, u32[]{:S(2)}) copy-start(bf16[128,512]{1,0:T(8,128)(2,1)} %param.21) | copy-start | bytes 393220
  38.8 6.2 %copy-start.9 = (u32[32]{0:T(128)S(1)}, u32[32]{0:T(128)}, u32[]{:S(2)}) copy-start(u32[32]{0:T(128)} %constant.89) | copy-start | bytes 388
  43.7 20.6 %copy-start.1 = (bf16[12,24,128]{2,1,0:T(8,128)(2,1)S(1)}, bf16[12,24,128]{2,1,0:T(8,128)(2,1)}, u32[]{:S(2)}) copy-start(bf16[12,24,128]{2,1,0:T(8,128)(2,1)} %param.14) | copy-start | bytes 221188
  44.7 61.9 %reduce-scatter.3.cloned.1.call-start = ((), (), s32[]{:S(2)}) async-start(), calls=%async_computation.2 | async-start | bytes 245760 | tf_op jit(solution)/shard_map/reduce_scatter | solution.py:121
  83.2 2.2 %copy-start.7 = (bf16[128,128]{1,0:T(8,128)(2,1)S(1)}, bf16[128,128]{1,0:T(8,128)(2,1)}, u32[]{:S(2)}) copy-start(bf16[128,128]{1,0:T(8,128)(2,1)} %param.22) | copy-start | bytes 98308
  84.2 25.7 %copy-start.5 = (bf16[128,128]{1,0:T(8,128)(2,1)S(1)}, bf16[128,128]{1,0:T(8,128)(2,1)}, u32[]{:S(2)}) copy-start(bf16[128,128]{1,0:T(8,128)(2,1)} %param.23) | copy-start | bytes 98308
  84.2 25.9 %copy-start.2 = (bf16[12,24,128]{2,1,0:T(8,128)(2,1)S(1)}, bf16[12,24,128]{2,1,0:T(8,128)(2,1)}, u32[]{:S(2)}) copy-start(bf16[12,24,128]{2,1,0:T(8,128)(2,1)} %all-reduce.3.cloned.1.call-done) | copy-start | bytes 221188
  84.2 26.4 %copy-start.3 = (bf16[128,512]{1,0:T(8,128)(2,1)S(1)}, bf16[128,512]{1,0:T(8,128)(2,1)}, u32[]{:S(2)}) copy-start(bf16[128,512]{1,0:T(8,128)(2,1)} %param.24) | copy-start | bytes 393220
Sparse Core Ops, SparseCore 0:
  44.8 19.3 all-reduce.2
  85.6 21.0 reduce-scatter.2
